TPU v7x, 32 devices: a whole 2x2x4 slice. The times are simulated.
32 devices in a mesh: heads: 2 (over y), ctx: 16 (over z, x, core).
Axes of the slice: x: 2, y: 2, z: 4, core: 2. Of those that a mesh axis runs over, the one named last changes fastest.
Arguments:
- queries: bfloat16 [8, 4096, 128], P('heads', 'ctx'), may hold values from -6 to 6
- key_rows: bfloat16 [8, 4096, 128], P('heads', 'ctx'), may hold values from -6 to 6
- value_rows: bfloat16 [8, 4096, 128], P('heads', 'ctx'), may hold values from -6 to 6
- level_weights: float32 [8, 13, 4096], P('heads', None, 'ctx'), may hold values from 0.1 to 3
- norm_gain: float32 [8, 128], P('heads'), may hold values from 0.1 to 1.9
- grad_normed: bfloat16 [8, 4096, 128], P('heads', 'ctx'), may hold values from -6 to 6
Outputs:
- normed: bfloat16 [8, 4096, 128], P('heads', 'ctx')
- grad_queries: bfloat16 [8, 4096, 128], P('heads', 'ctx')
- grad_keys: bfloat16 [8, 4096, 128], P('heads', 'ctx')
- grad_values: bfloat16 [8, 4096, 128], P('heads', 'ctx')
- grad_level_weights: float32 [8, 13, 4096], P('heads', None, 'ctx')
All inputs are finite; a program needn't handle non-finite values.
Results may differ from a plain program's by a relative error of at most 0.006.
Values sent between devices are 32-bit elements; how exact they have to be, the bound alone decides.
A program may use at most 64 MiB of HBM per device.

v0:
```python
import math
import jax
import jax.numpy as jnp
from jax import lax
from jax.sharding import PartitionSpec as P

EPS = 1e-06
HIGH = lax.Precision.HIGHEST


def from_partner(value, axis, bit):
    mask = 2**bit
    pairs = [(source, source ^ mask) for source in range(lax.axis_size(axis))]
    return lax.ppermute(value, axis, pairs)


def level_scale(number, head_dim):
    return 2.0 ** (-max(number - 1, 0) / 2.0) / math.sqrt(head_dim)


def level_matrix(count):
    position = jnp.arange(count, dtype=jnp.int32)
    differ = jnp.bitwise_xor(position[:, None], position[None, :])
    bucket = jnp.zeros((count, count), jnp.int32)
    for exponent in range(count.bit_length() - 1):
        bucket = bucket + (differ >= 2**exponent).astype(jnp.int32)
    causal = position[None, :] <= position[:, None]
    return (bucket, causal)


def near_weights(factors, bucket, causal, head_dim):
    weights = jnp.zeros(factors[0].shape + (bucket.shape[1],), jnp.float32)
    for number in range(len(factors)):
        scaled = factors[number] * level_scale(number, head_dim)
        weights = weights + jnp.where(
            (bucket == number) & causal, scaled[..., None], jnp.float32(0.0)
        )
    return weights


def pair_level(matrix, step_bit):
    return from_partner(matrix, "ctx", step_bit)


def shards(queries, key_rows, value_rows, level_weights, norm_gain, grad_normed):
    heads_here, tokens_here, head_dim = queries.shape
    local_levels = tokens_here.bit_length()
    far_levels = lax.axis_size("ctx").bit_length() - 1
    block_index = lax.axis_index("ctx")
    width = heads_here * lax.axis_size("heads") * head_dim
    key_value = jnp.einsum("hsd,hse->hde", key_rows, value_rows, preferred_element_type=jnp.float32)
    group_sum = key_value
    far_list = []
    for step_bit in range(far_levels):
        partner = from_partner(group_sum, "ctx", step_bit)
        bit_set = block_index >> step_bit & 1
        far_list.append(jnp.where(bit_set == 1, partner, jnp.float32(0.0)))
        group_sum = group_sum + partner
    states = jnp.stack(far_list, 0)
    bucket, causal = level_matrix(tokens_here)
    weights = near_weights(
        [level_weights[:, number, :] for number in range(local_levels)], bucket, causal, head_dim
    )
    scores = jnp.einsum("htd,hsd->hts", queries, key_rows, preferred_element_type=jnp.float32)
    weighted = (weights * scores).astype(jnp.bfloat16)
    near_out = jnp.einsum("hts,hse->hte", weighted, value_rows, preferred_element_type=jnp.float32)
    far_scale = jnp.stack(
        [
            level_weights[:, local_levels + depth, :] * level_scale(local_levels + depth, head_dim)
            for depth in range(far_levels)
        ],
        0,
    )
    query_wide = queries.astype(jnp.float32)
    far_terms = jnp.einsum("htd,mhde->mhte", query_wide, states, precision=HIGH)
    attended = near_out + jnp.sum(far_scale[..., None] * far_terms, 0)
    totals = lax.psum(jnp.sum(attended * attended, axis=(0, 2)), "heads")
    inv_rms = lax.rsqrt(totals / width + EPS)
    normed = (attended * inv_rms[None, :, None] * norm_gain[:, None, :]).astype(jnp.bfloat16)
    scaled = norm_gain[:, None, :] * grad_normed.astype(jnp.float32)
    inner_sum = lax.psum(jnp.sum(scaled * attended, axis=(0, 2)), "heads")
    grad_out = (
        inv_rms[None, :, None] * scaled - attended * (inv_rms**3 * inner_sum / width)[None, :, None]
    ).astype(jnp.bfloat16)
    grad_wide = grad_out.astype(jnp.float32)
    grad_mix = jnp.einsum("hte,hse->hts", grad_out, value_rows, preferred_element_type=jnp.float32)
    product = grad_mix * scores
    near_grads = [
        level_scale(number, head_dim)
        * jnp.sum(jnp.where((bucket == number) & causal, product, jnp.float32(0.0)), axis=2)
        for number in range(local_levels)
    ]
    far_grads = [
        level_scale(local_levels + depth, head_dim) * jnp.sum(grad_wide * far_terms[depth], axis=2)
        for depth in range(far_levels)
    ]
    grad_scores = (weights * grad_mix).astype(jnp.bfloat16)
    grad_q = jnp.einsum("hts,hsd->htd", grad_scores, key_rows, preferred_element_type=jnp.float32)
    grad_q = grad_q + jnp.sum(
        far_scale[..., None] * jnp.einsum("hte,mhde->mhtd", grad_wide, states, precision=HIGH), 0
    )
    scaled_queries = (far_scale[..., None] * queries[None]).astype(jnp.bfloat16)
    grad_states = jnp.einsum(
        "mhtd,hte->mhde", scaled_queries, grad_out, preferred_element_type=jnp.float32
    )
    grad_kv = jnp.zeros((heads_here, head_dim, head_dim), jnp.float32)
    for depth in range(far_levels):
        level_total = grad_states[depth]
        for step_bit in range(depth + 1):
            partner = pair_level(level_total, step_bit)
            if step_bit < depth:
                level_total = level_total + partner
            else:
                bit_set = block_index >> step_bit & 1
                grad_kv = grad_kv + jnp.where(bit_set == 0, partner, jnp.float32(0.0))
    grad_kv = grad_kv.astype(jnp.bfloat16)
    grad_k = jnp.einsum("hts,htd->hsd", grad_scores, queries, preferred_element_type=jnp.float32)
    grad_k = grad_k + jnp.einsum(
        "hse,hde->hsd", value_rows, grad_kv, preferred_element_type=jnp.float32
    )
    grad_v = jnp.einsum("hts,hte->hse", weighted, grad_out, preferred_element_type=jnp.float32)
    grad_v = grad_v + jnp.einsum(
        "hsd,hde->hse", key_rows, grad_kv, preferred_element_type=jnp.float32
    )
    grad_rates = jnp.stack(near_grads + far_grads, axis=1)
    return (
        normed,
        grad_q.astype(jnp.bfloat16),
        grad_k.astype(jnp.bfloat16),
        grad_v.astype(jnp.bfloat16),
        grad_rates,
    )


def solution(mesh):
    in_specs = (
        P("heads", "ctx", None),
        P("heads", "ctx", None),
        P("heads", "ctx", None),
        P("heads", None, "ctx"),
        P("heads", None),
        P("heads", "ctx", None),
    )
    out_specs = (
        P("heads", "ctx", None),
        P("heads", "ctx", None),
        P("heads", "ctx", None),
        P("heads", "ctx", None),
        P("heads", None, "ctx"),
    )
    return jax.shard_map(shards, mesh=mesh, in_specs=in_specs, out_specs=out_specs, check_vma=False)
```

profile of v0, /device:TPU:0, one launch (start us, length us, event | category | flops | bytes accessed | tf_op | source)
XLA Modules:
  0.0 86.8 jit_solution(17006751572486609093)
XLA Ops:
  0.6 0.0 copy-start
  0.7 0.9 %copy-done = bf16[4,256,128]{2,1,0:T(8,128)(2,1)S(1)} copy-done((bf16[4,256,128]{2,1,0:T(8,128)(2,1)S(1)}, bf16[4,256,128]{2,1,0:T(8,128)(2,1)}, u32[]{:S(2)}) %copy-start) | copy-done | bytes 262168
  1.6 1.2 %fusion.39 = f32[4,128,128]{2,1,0:T(8,128)S(1)} fusion(bf16[4,256,128]{2,1,0:T(8,128)(2,1)} %param.7, bf16[4,256,128]{2,1,0:T(8,128)(2,1)S(1)} %copy-done), kind=kOutput, calls=%fused_computation.115 | convolution fusion | flops 33554432 | bytes 786432 | tf_op jit(solution)/shard_map/hsd,hse->hde/dot_general | solution.py:51
  2.8 0.6 collective-permute-start
  3.4 0.2 fusion.20
  3.5 0.2 fusion.22
  3.7 0.8 collective-permute-done
  4.6 0.0 copy-start.9
  4.6 0.0 copy-start.1
  4.6 2.9 %collective-permute-start.1 = (f32[4,128,128]{2,1,0:T(8,128)S(1)}, f32[4,128,128]{2,1,0:T(8,128)S(1)}, u32[]{:S(2)}, u32[]{:S(2)}) collective-permute-start(f32[4,128,128]{2,1,0:T(8,128)S(1)} %get-tuple-element.42), channel_id=1, source_target_pairs={{0,2},{1,3},{2,0},{3,1},{4,6},{5,7},{6,4},{7,5},{8,10},{9,11},{10,... | collective-permute-start | bytes 786440 | tf_op jit(solution)/shard_map/ppermute | solution.py:14
  7.5 0.1 fusion.28
  7.7 0.0 copy-start.34
  7.8 6.3 %collective-permute-done.1 = f32[4,128,128]{2,1,0:T(8,128)S(1)} collective-permute-done((f32[4,128,128]{2,1,0:T(8,128)S(1)}, f32[4,128,128]{2,1,0:T(8,128)S(1)}, u32[]{:S(2)}, u32[]{:S(2)}) %collective-permute-start.1) | collective-permute-done | bytes 262176 | tf_op jit(solution)/shard_map/ppermute | solution.py:14
  14.1 0.7 select_bitcast_fusion.2
  14.9 1.8 %collective-permute-start.2 = (f32[4,128,128]{2,1,0:T(8,128)S(1)}, f32[4,128,128]{2,1,0:T(8,128)S(1)}, u32[]{:S(2)}, u32[]{:S(2)}) collective-permute-start(f32[4,128,128]{2,1,0:T(8,128)S(1)} %get-tuple-element.44), channel_id=1, source_target_pairs={{0,4},{1,5},{2,6},{3,7},{4,0},{5,1},{6,2},{7,3},{8,12},{9,13},{10,... | collective-permute-start | bytes 786440 | tf_op jit(solution)/shard_map/ppermute | solution.py:14
  16.7 0.1 copy.35
  16.9 0.9 %copy.42 = f32[4,256,128]{1,2,0:T(8,128)} copy(bf16[4,256,128]{2,1,0:T(8,128)(2,1)S(1)} %copy-done.2) | data formatting | bytes 786432 | tf_op jit(solution)/shard_map/convert_element_type | solution.py:102
  17.8 0.2 fusion.24
  18.0 0.2 fusion.26
  18.2 4.5 %collective-permute-done.2 = f32[4,128,128]{2,1,0:T(8,128)S(1)} collective-permute-done((f32[4,128,128]{2,1,0:T(8,128)S(1)}, f32[4,128,128]{2,1,0:T(8,128)S(1)}, u32[]{:S(2)}, u32[]{:S(2)}) %collective-permute-start.2) | collective-permute-done | bytes 262176 | tf_op jit(solution)/shard_map/ppermute | solution.py:14
  22.7 0.0 copy-start.13
  22.7 2.6 %collective-permute-start.3 = (f32[4,128,128]{2,1,0:T(8,128)S(1)}, f32[4,128,128]{2,1,0:T(8,128)S(1)}, u32[]{:S(2)}, u32[]{:S(2)}) collective-permute-start(f32[4,128,128]{2,1,0:T(8,128)S(1)} %get-tuple-element.46), channel_id=1, source_target_pairs={{0,8},{1,9},{2,10},{3,11},{4,12},{5,13},{6,14},{7,15},{8,0},{9,1},... | collective-permute-start | bytes 786440 | tf_op jit(solution)/shard_map/ppermute | solution.py:14
  25.3 2.0 %multiply_convert_fusion.3 = (bf16[4,256,256]{1,2,0:T(8,128)(2,1)S(1)}, f32[4,256,256]{1,2,0:T(8,128)}) fusion(f32[4,256]{1,0:T(4,128)S(1)} %get-tuple-element.50, pred[256,256]{0,1:T(8,128)(4,1)S(1)} %get-tuple-element.69, f32[4,256]{1,0:T(4,128)S(1)} %get-tuple-element.51, pred[256,256]{0,1:T(8,128)(4,1)S(1)} %get-tuple-element.70, ...), kind=kOutput, calls=%fused_computation.28 | convolution fusion | flops 72089600 | bytes 2723840 | tf_op jit(solution)/shard_map/htd,hsd->hts/dot_general | solution.py:64
  27.5 8.7 %collective-permute-done.3 = f32[4,128,128]{2,1,0:T(8,128)S(1)} collective-permute-done((f32[4,128,128]{2,1,0:T(8,128)S(1)}, f32[4,128,128]{2,1,0:T(8,128)S(1)}, u32[]{:S(2)}, u32[]{:S(2)}) %collective-permute-start.3) | collective-permute-done | bytes 262176 | tf_op jit(solution)/shard_map/ppermute | solution.py:14
  36.2 0.0 copy-start.7
  36.2 0.0 copy-start.32
  36.3 1.1 %multiply_reduce_fusion = (f32[4,256,128]{1,2,0:T(8,128)S(1)}, f32[4,4,256,128]{2,3,1,0:T(8,128)S(1)}) fusion(f32[4,4,256]{2,1,0:T(4,128)S(1)} %pad_maximum_fusion.3, bf16[4,256,128]{2,1,0:T(8,128)(2,1)S(1)} %copy-done.2, f32[1,4,128,128]{3,2,1,0:T(8,128)S(1)} %select_bitcast_fusion, f32[1,4,128,128]{3,2,1,0:T(8,128)S(1)} %get-tuple-element.45, ...), kind=kOutput, calls=%fused_computation.3 | convolution fusion | flops 807010304 | bytes 3948544 | tf_op jit(solution)/shard_map/htd,mhde->mhte/dot_general | solution.py:75
  37.4 1.1 %multiply_reduce_fusion.1 = (f32[256]{0:T(256)S(1)}, f32[256]{0:T(256)S(1)}, f32[4,256,128]{1,2,0:T(8,128)}) fusion(bf16[4,256,128]{1,2,0:T(8,128)(2,1)S(1)} %copy.35, f32[4,128]{1,0:T(4,128)S(1)} %copy-done.32, f32[4,256,128]{1,2,0:T(8,128)S(1)} %get-tuple-element.62, bf16[4,256,256]{1,2,0:T(8,128)(2,1)S(1)} %get-tuple-element.64, ...), kind=kOutput, calls=%fused_computation.43 | convolution fusion | flops 68025856 | bytes 2101248 | tf_op jit(solution)/shard_map/hts,hse->hte/dot_general | solution.py:66
  38.6 4.9 %all-reduce = (f32[256]{0:T(256)S(1)}, f32[256]{0:T(256)S(1)}) all-reduce(f32[256]{0:T(256)S(1)} %get-tuple-element.29, f32[256]{0:T(256)S(1)} %get-tuple-element.28), channel_id=1, replica_groups=mesh['heads'=2,'ctx'=16] {'heads'}, use_global_device_ids=true, to_apply=%region_2.3 | all-reduce | flops 512 | bytes 4096 | tf_op jit(solution)/shard_map/psum | solution.py:77
  43.5 1.4 %fusion.11 = (f32[4,256]{1,0:T(4,128)S(1)}, f32[4,256]{1,0:T(4,128)S(1)}, f32[4,256]{1,0:T(4,128)S(1)}, f32[4,256]{1,0:T(4,128)S(1)}, bf16[4,256,128]{1,2,0:T(8,128)(2,1)S(1)}, /*index=5*/bf16[4,256,128]{1,2,0:T(8,128)(2,1)S(1)}) fusion(f32[4,4,256,128]{2,3,1,0:T(8,128)S(1)} %get-tuple-element.63, f32[4,256,128]{1,2,0:T(8,128)} %get-tuple-element.66, ...), kind=kLoop, calls=%fused_computation.37 | loop fusion | flops 2355200 | bytes 3428352 | tf_op jit(solution)/shard_map/reduce_sum | solution.py:94
  45.0 2.3 %multiply_convert_fusion.2 = (bf16[4,256,256]{1,2,0:T(8,128)(2,1)S(1)}, f32[4,256,256]{1,2,0:T(8,128)S(1)}) fusion(f32[4,256]{1,0:T(4,128)} %copy-done.34, pred[256,256]{0,1:T(8,128)(4,1)S(1)} %get-tuple-element.69, f32[4,256]{1,0:T(4,128)} %copy-done.35, pred[256,256]{0,1:T(8,128)(4,1)S(1)} %get-tuple-element.70, f32[4,256]{1,0:T(4,128)} %copy-done.36, ...), kind=kOutput, calls=%fused_computation.26 | convolution fusion | flops 72089600 | bytes 2723840 | tf_op jit(solution)/shard_map/hte,hse->hts/dot_general | solution.py:86
  47.4 0.9 %select_reduce_fusion = (f32[4,256]{1,0:T(4,128)S(1)}, f32[4,256]{1,0:T(4,128)S(1)}, f32[4,256]{1,0:T(4,128)S(1)}, f32[4,256]{1,0:T(4,128)S(1)}, f32[4,256]{1,0:...) fusion(pred[256,256]{0,1:T(8,128)(4,1)S(1)} %get-tuple-element.69, ...), kind=kLoop, calls=%fused_computation.16 | loop fusion | flops 4971520 | bytes 2723840 | tf_op jit(solution)/shard_map/reduce_sum | solution.py:90
  48.3 0.0 copy-done.3
  48.3 0.4 convolution_bitcast_fusion.1
  48.8 0.8 slice_bitcast_fusion.7
  49.6 0.5 collective-permute-start.5
  50.1 0.5 collective-permute-start.4
  50.7 0.0 copy-start.8
  50.7 0.0 copy-start.10
  50.7 0.0 copy-start.14
  50.7 0.4 collective-permute-done.10
  51.1 0.4 collective-permute-done.5
  51.5 0.4 collective-permute-done.7
  51.8 0.8 fusion.36
  52.6 1.2 %collective-permute-start.11 = (f32[4,128,128]{2,1,0:T(8,128)S(1)}, f32[4,128,128]{2,1,0:T(8,128)S(1)}, u32[]{:S(2)}, u32[]{:S(2)}) collective-permute-start(f32[4,128,128]{2,1,0:T(8,128)S(1)} %get-tuple-element.38), channel_id=1, source_target_pairs={{0,2},{1,3},{2,0},{3,1},{4,6},{5,7},{6,4},{7,5},{8,10},{9,11},{10,... | collective-permute-start | bytes 786440 | tf_op jit(solution)/shard_map/ppermute | solution.py:14
  53.8 0.3 fusion.41
  54.1 0.9 %collective-permute-start.8 = (f32[4,128,128]{2,1,0:T(8,128)S(1)}, f32[4,128,128]{2,1,0:T(8,128)}, u32[]{:S(2)}, u32[]{:S(2)}) collective-permute-start(f32[4,128,128]{2,1,0:T(8,128)S(1)} %get-tuple-element.39), channel_id=1, source_target_pairs={{0,2},{1,3},{2,0},{3,1},{4,6},{5,7},{6,4},{7,5},{8,10},{9,11},{10,... | collective-permute-start | bytes 786440 | tf_op jit(solution)/shard_map/ppermute | solution.py:14
  55.0 6.8 %collective-permute-done.11 = f32[4,128,128]{2,1,0:T(8,128)S(1)} collective-permute-done((f32[4,128,128]{2,1,0:T(8,128)S(1)}, f32[4,128,128]{2,1,0:T(8,128)S(1)}, u32[]{:S(2)}, u32[]{:S(2)}) %collective-permute-start.11) | collective-permute-done | bytes 262176 | tf_op jit(solution)/shard_map/ppermute | solution.py:14
  61.8 0.4 collective-permute-start.12
  62.3 1.8 %fusion = f32[4,256,128]{1,2,0:T(8,128)} fusion(f32[4,4,256]{2,1,0:T(4,128)S(1)} %pad_maximum_fusion.3, f32[1,4,128,128]{3,2,1,0:T(8,128)S(1)} %copy-done.8, f32[1,4,128,128]{3,2,1,0:T(8,128)S(1)} %copy-done.14, f32[1,4,128,128]{3,2,1,0:T(8,128)S(1)} %copy-done.12, f32[1,4,128,128]{3,2,1,0:T(8,128)S(1)} %copy-done.10, ...), kind=kOutput, calls=%fused_computation.1 | convolution fusion | flops 807010304 | bytes 1851392 | tf_op jit(solution)/shard_map/hte,mhde->mhtd/dot_general | solution.py:100
  64.1 1.3 %copy.41 = f32[4,256,128]{2,1,0:T(8,128)S(1)} copy(f32[4,256,128]{1,2,0:T(8,128)} %fusion) | data formatting | bytes 1048576 | tf_op jit(solution)/shard_map/reduce_sum | solution.py:99
  65.4 0.8 copy.49
  66.3 0.3 fusion.40
  66.6 1.6 %collective-permute-start.6 = (f32[4,128,128]{2,1,0:T(8,128)S(1)}, f32[4,128,128]{2,1,0:T(8,128)S(1)}, u32[]{:S(2)}, u32[]{:S(2)}) collective-permute-start(f32[4,128,128]{2,1,0:T(8,128)S(1)} %copy-done.15), channel_id=1, source_target_pairs={{0,2},{1,3},{2,0},{3,1},{4,6},{5,7},{6,4},{7,5},{8,10},{9,11},{10,... | collective-permute-start | bytes 786440 | tf_op jit(solution)/shard_map/ppermute | solution.py:14
  68.1 1.0 %add.366 = f32[4,128,128]{2,1,0:T(8,128)S(1)} add(f32[4,128,128]{2,1,0:T(8,128)S(1)} %get-tuple-element.39, f32[4,128,128]{2,1,0:T(8,128)} %collective-permute-done.8) | non-fusion elementwise | flops 65536 | bytes 786432 | tf_op jit(solution)/shard_map/add | solution.py:112
  69.1 1.4 %collective-permute-start.9 = (f32[4,128,128]{2,1,0:T(8,128)S(1)}, f32[4,128,128]{2,1,0:T(8,128)S(1)}, u32[]{:S(2)}, u32[]{:S(2)}) collective-permute-start(f32[4,128,128]{2,1,0:T(8,128)S(1)} %add.366), channel_id=1, source_target_pairs={{0,4},{1,5},{2,6},{3,7},{4,0},{5,1},{6,2},{7,3},{8,12},{9,13},{10,... | collective-permute-start | bytes 786440 | tf_op jit(solution)/shard_map/ppermute | solution.py:14
  70.5 1.0 %add.370 = f32[4,128,128]{2,1,0:T(8,128)S(1)} add(f32[4,128,128]{2,1,0:T(8,128)S(1)} %add.369, f32[4,128,128]{2,1,0:T(8,128)} %collective-permute-done.12) | non-fusion elementwise | flops 65536 | bytes 786432 | tf_op jit(solution)/shard_map/add | solution.py:112
  71.5 2.1 %collective-permute-start.13 = (f32[4,128,128]{2,1,0:T(8,128)S(1)}, f32[4,128,128]{2,1,0:T(8,128)S(1)}, u32[]{:S(2)}, u32[]{:S(2)}) collective-permute-start(f32[4,128,128]{2,1,0:T(8,128)S(1)} %add.370), channel_id=1, source_target_pairs={{0,8},{1,9},{2,10},{3,11},{4,12},{5,13},{6,14},{7,15},{8,0},{9,1},... | collective-permute-start | bytes 786440 | tf_op jit(solution)/shard_map/ppermute | solution.py:14
  73.6 1.0 %fusion.3 = bf16[4,256,128]{2,1,0:T(8,128)(2,1)} fusion(f32[4,256,128]{2,1,0:T(8,128)S(1)} %copy.41, bf16[4,256,256]{1,2,0:T(8,128)(2,1)S(1)} %get-tuple-element.67, bf16[4,256,128]{2,1,0:T(8,128)(2,1)S(1)} %copy-done.1), kind=kOutput, calls=%fused_computation.12 | convolution fusion | flops 67371008 | bytes 1572864 | tf_op jit(solution)/shard_map/hts,hsd->htd/dot_general | solution.py:98
  74.7 5.8 %collective-permute-done.9 = f32[4,128,128]{2,1,0:T(8,128)S(1)} collective-permute-done((f32[4,128,128]{2,1,0:T(8,128)S(1)}, f32[4,128,128]{2,1,0:T(8,128)S(1)}, u32[]{:S(2)}, u32[]{:S(2)}) %collective-permute-start.9) | collective-permute-done | bytes 262176 | tf_op jit(solution)/shard_map/ppermute | solution.py:14
  80.5 3.4 %collective-permute-done.13 = f32[4,128,128]{2,1,0:T(8,128)S(1)} collective-permute-done((f32[4,128,128]{2,1,0:T(8,128)S(1)}, f32[4,128,128]{2,1,0:T(8,128)S(1)}, u32[]{:S(2)}, u32[]{:S(2)}) %collective-permute-start.13) | collective-permute-done | bytes 262176 | tf_op jit(solution)/shard_map/ppermute | solution.py:14
  84.0 1.0 %add_convert_fusion = bf16[4,128,128]{2,1,0:T(8,128)(2,1)S(1)} fusion(f32[4,128,128]{2,1,0:T(8,128)S(1)} %collective-permute-done.13, f32[4,128,128]{2,1,0:T(8,128)S(1)} %collective-permute-done.9, f32[4,128,128]{2,1,0:T(8,128)S(1)} %collective-permute-done.6, f32[4,128,128]{2,1,0:T(8,128)} %collective-permute-done.4, pred[]{:T(512)S(6)} %eq.94, ...), kind=kLoop, calls=%fused_computation.73 | loop fusion | flops 524288 | bytes 1179652 | tf_op jit(solution)/shard_map/convert_element_type | solution.py:116
  85.0 0.9 %fusion.4 = bf16[4,256,128]{2,1,0:T(8,128)(2,1)} fusion(f32[4,256,128]{2,1,0:T(8,128)S(1)} %fusion.41, bf16[4,256,128]{2,1,0:T(8,128)(2,1)S(1)} %copy-done.1, bf16[4,128,128]{2,1,0:T(8,128)(2,1)S(1)} %add_convert_fusion), kind=kOutput, calls=%fused_computation.13 | convolution fusion | flops 33816576 | bytes 1179648 | tf_op jit(solution)/shard_map/hsd,hde->hse/dot_general | solution.py:122
  85.9 0.9 %fusion.5 = bf16[4,256,128]{2,1,0:T(8,128)(2,1)} fusion(f32[4,256,128]{2,1,0:T(8,128)S(1)} %fusion.40, bf16[4,128,128]{2,1,0:T(8,128)(2,1)S(1)} %add_convert_fusion, bf16[4,256,128]{2,1,0:T(8,128)(2,1)S(1)} %copy-done), kind=kOutput, calls=%fused_computation.14 | convolution fusion | flops 33816576 | bytes 1179648 | tf_op jit(solution)/shard_map/hse,hde->hsd/dot_general | solution.py:118
  (100 shorter events, 0.5 us)
Async XLA Ops:
  0.6 1.0 %copy-start = (bf16[4,256,128]{2,1,0:T(8,128)(2,1)S(1)}, bf16[4,256,128]{2,1,0:T(8,128)(2,1)}, u32[]{:S(2)}) copy-start(bf16[4,256,128]{2,1,0:T(8,128)(2,1)} %param.8) | copy-start | bytes 786436
  0.6 7.0 %copy-start.31 = (f32[4,13,256]{2,0,1:T(4,128)S(1)}, f32[4,13,256]{2,0,1:T(4,128)}, u32[]{:S(2)}) copy-start(f32[4,13,256]{2,0,1:T(4,128)} %param.9) | copy-start | bytes 159748
  0.7 16.0 %copy-start.30 = (bf16[4,256,128]{2,1,0:T(8,128)(2,1)S(1)}, bf16[4,256,128]{2,1,0:T(8,128)(2,1)}, u32[]{:S(2)}) copy-start(bf16[4,256,128]{2,1,0:T(8,128)(2,1)} %param.11) | copy-start | bytes 786436
  0.7 16.2 %copy-start.2 = (bf16[4,256,128]{2,1,0:T(8,128)(2,1)S(1)}, bf16[4,256,128]{2,1,0:T(8,128)(2,1)}, u32[]{:S(2)}) copy-start(bf16[4,256,128]{2,1,0:T(8,128)(2,1)} %param.6) | copy-start | bytes 786436
  2.8 1.7 %collective-permute-start = (f32[4,128,128]{2,1,0:T(8,128)S(1)}, f32[4,128,128]{2,1,0:T(8,128)S(1)}, u32[]{:S(2)}, u32[]{:S(2)}) collective-permute-start(f32[4,128,128]{2,1,0:T(8,128)S(1)} %fusion.39), channel_id=1, source_target_pairs={{0,1},{1,0},{2,3},{3,2},{4,5},{5,4},{6,7},{7,6},{8,9},{9,8},{10,11... | collective-permute-start | bytes 786440 | tf_op jit(solution)/shard_map/ppermute | solution.py:14
  3.7 23.6 %copy-start.16 = (pred[256,256]{0,1:T(8,128)(4,1)}, pred[256,256]{0,1:T(8,128)(4,1)S(1)}, u32[]{:S(2)}) copy-start(pred[256,256]{0,1:T(8,128)(4,1)S(1)} %get-tuple-element.71) | copy-start | bytes 196612
  3.7 23.6 %copy-start.18 = (pred[256,256]{0,1:T(8,128)(4,1)}, pred[256,256]{0,1:T(8,128)(4,1)S(1)}, u32[]{:S(2)}) copy-start(pred[256,256]{0,1:T(8,128)(4,1)S(1)} %get-tuple-element.72) | copy-start | bytes 196612
  4.6 31.7 %copy-start.9 = (f32[1,4,128,128]{3,2,1,0:T(8,128)}, f32[1,4,128,128]{3,2,1,0:T(8,128)S(1)}, u32[]{:S(2)}) copy-start(f32[1,4,128,128]{3,2,1,0:T(8,128)S(1)} %get-tuple-element.41) | copy-start | bytes 786436
  4.6 20.7 %copy-start.1 = (bf16[4,256,128]{2,1,0:T(8,128)(2,1)S(1)}, bf16[4,256,128]{2,1,0:T(8,128)(2,1)}, u32[]{:S(2)}) copy-start(bf16[4,256,128]{2,1,0:T(8,128)(2,1)} %param.7) | copy-start | bytes 786436
  4.6 9.5 %collective-permute-start.1 = (f32[4,128,128]{2,1,0:T(8,128)S(1)}, f32[4,128,128]{2,1,0:T(8,128)S(1)}, u32[]{:S(2)}, u32[]{:S(2)}) collective-permute-start(f32[4,128,128]{2,1,0:T(8,128)S(1)} %get-tuple-element.42), channel_id=1, source_target_pairs={{0,2},{1,3},{2,0},{3,1},{4,6},{5,7},{6,4},{7,5},{8,10},{9,11},{10,... | collective-permute-start | bytes 786440 | tf_op jit(solution)/shard_map/ppermute | solution.py:14
  7.6 19.7 %copy-start.20 = (pred[256,256]{0,1:T(8,128)(4,1)}, pred[256,256]{0,1:T(8,128)(4,1)S(1)}, u32[]{:S(2)}) copy-start(pred[256,256]{0,1:T(8,128)(4,1)S(1)} %fusion.28) | copy-start | bytes 196612
  7.7 19.7 %copy-start.33 = (f32[4,256]{1,0:T(4,128)}, f32[4,256]{1,0:T(4,128)S(1)}, u32[]{:S(2)}) copy-start(f32[4,256]{1,0:T(4,128)S(1)} %get-tuple-element.47) | copy-start | bytes 12292
  7.7 19.6 %copy-start.34 = (f32[4,256]{1,0:T(4,128)}, f32[4,256]{1,0:T(4,128)S(1)}, u32[]{:S(2)}) copy-start(f32[4,256]{1,0:T(4,128)S(1)} %get-tuple-element.50) | copy-start | bytes 12292
  7.7 19.6 %copy-start.35 = (f32[4,256]{1,0:T(4,128)}, f32[4,256]{1,0:T(4,128)S(1)}, u32[]{:S(2)}) copy-start(f32[4,256]{1,0:T(4,128)S(1)} %get-tuple-element.51) | copy-start | bytes 12292
  7.7 19.6 %copy-start.36 = (f32[4,256]{1,0:T(4,128)}, f32[4,256]{1,0:T(4,128)S(1)}, u32[]{:S(2)}) copy-start(f32[4,256]{1,0:T(4,128)S(1)} %get-tuple-element.52) | copy-start | bytes 12292
  7.7 19.6 %copy-start.37 = (f32[4,256]{1,0:T(4,128)}, f32[4,256]{1,0:T(4,128)S(1)}, u32[]{:S(2)}) copy-start(f32[4,256]{1,0:T(4,128)S(1)} %get-tuple-element.53) | copy-start | bytes 12292
  7.7 19.6 %copy-start.38 = (f32[4,256]{1,0:T(4,128)}, f32[4,256]{1,0:T(4,128)S(1)}, u32[]{:S(2)}) copy-start(f32[4,256]{1,0:T(4,128)S(1)} %get-tuple-element.54) | copy-start | bytes 12292
  7.8 19.6 %copy-start.39 = (f32[4,256]{1,0:T(4,128)}, f32[4,256]{1,0:T(4,128)S(1)}, u32[]{:S(2)}) copy-start(f32[4,256]{1,0:T(4,128)S(1)} %get-tuple-element.55) | copy-start | bytes 12292
  7.8 19.6 %copy-start.40 = (f32[4,256]{1,0:T(4,128)}, f32[4,256]{1,0:T(4,128)S(1)}, u32[]{:S(2)}) copy-start(f32[4,256]{1,0:T(4,128)S(1)} %get-tuple-element.56) | copy-start | bytes 12292
  7.8 19.6 %copy-start.41 = (f32[4,256]{1,0:T(4,128)}, f32[4,256]{1,0:T(4,128)S(1)}, u32[]{:S(2)}) copy-start(f32[4,256]{1,0:T(4,128)S(1)} %get-tuple-element.57) | copy-start | bytes 12292
  14.9 7.8 %collective-permute-start.2 = (f32[4,128,128]{2,1,0:T(8,128)S(1)}, f32[4,128,128]{2,1,0:T(8,128)S(1)}, u32[]{:S(2)}, u32[]{:S(2)}) collective-permute-start(f32[4,128,128]{2,1,0:T(8,128)S(1)} %get-tuple-element.44), channel_id=1, source_target_pairs={{0,4},{1,5},{2,6},{3,7},{4,0},{5,1},{6,2},{7,3},{8,12},{9,13},{10,... | collective-permute-start | bytes 786440 | tf_op jit(solution)/shard_map/ppermute | solution.py:14
  18.0 9.5 %copy-start.22 = (pred[256,256]{0,1:T(8,128)(4,1)}, pred[256,256]{0,1:T(8,128)(4,1)S(1)}, u32[]{:S(2)}) copy-start(pred[256,256]{0,1:T(8,128)(4,1)S(1)} %get-tuple-element.73) | copy-start | bytes 196612
  18.0 9.5 %copy-start.24 = (pred[256,256]{0,1:T(8,128)(4,1)}, pred[256,256]{0,1:T(8,128)(4,1)S(1)}, u32[]{:S(2)}) copy-start(pred[256,256]{0,1:T(8,128)(4,1)S(1)} %get-tuple-element.74) | copy-start | bytes 196612
  18.1 9.3 %copy-start.26 = (pred[256,256]{0,1:T(8,128)(4,1)}, pred[256,256]{0,1:T(8,128)(4,1)S(1)}, u32[]{:S(2)}) copy-start(pred[256,256]{0,1:T(8,128)(4,1)S(1)} %get-tuple-element.75) | copy-start | bytes 196612
  18.2 9.3 %copy-start.28 = (pred[256,256]{0,1:T(8,128)(4,1)}, pred[256,256]{0,1:T(8,128)(4,1)S(1)}, u32[]{:S(2)}) copy-start(pred[256,256]{0,1:T(8,128)(4,1)S(1)} %get-tuple-element.76) | copy-start | bytes 196612
  22.7 13.6 %copy-start.13 = (f32[1,4,128,128]{3,2,1,0:T(8,128)}, f32[1,4,128,128]{3,2,1,0:T(8,128)S(1)}, u32[]{:S(2)}) copy-start(f32[1,4,128,128]{3,2,1,0:T(8,128)S(1)} %get-tuple-element.45) | copy-start | bytes 786436
  22.7 13.5 %collective-permute-start.3 = (f32[4,128,128]{2,1,0:T(8,128)S(1)}, f32[4,128,128]{2,1,0:T(8,128)S(1)}, u32[]{:S(2)}, u32[]{:S(2)}) collective-permute-start(f32[4,128,128]{2,1,0:T(8,128)S(1)} %get-tuple-element.46), channel_id=1, source_target_pairs={{0,8},{1,9},{2,10},{3,11},{4,12},{5,13},{6,14},{7,15},{8,0},{9,1},... | collective-permute-start | bytes 786440 | tf_op jit(solution)/shard_map/ppermute | solution.py:14
  25.3 10.9 %copy-start.11 = (f32[1,4,128,128]{3,2,1,0:T(8,128)S(1)}, f32[1,4,128,128]{3,2,1,0:T(8,128)}, u32[]{:S(2)}) copy-start(f32[1,4,128,128]{3,2,1,0:T(8,128)} %get-tuple-element.43) | copy-start | bytes 786436
  27.5 9.9 %copy-start.4 = (bf16[4,256,256]{1,2,0:T(8,128)(2,1)}, bf16[4,256,256]{1,2,0:T(8,128)(2,1)S(1)}, u32[]{:S(2)}) copy-start(bf16[4,256,256]{1,2,0:T(8,128)(2,1)S(1)} %get-tuple-element.64) | copy-start | bytes 1572868
  36.2 2.3 %copy-start.7 = (f32[1,4,128,128]{3,2,1,0:T(8,128)}, f32[1,4,128,128]{3,2,1,0:T(8,128)S(1)}, u32[]{:S(2)}) copy-start(f32[1,4,128,128]{3,2,1,0:T(8,128)S(1)} %select_bitcast_fusion) | copy-start | bytes 786436
  36.2 1.2 %copy-start.32 = (f32[4,128]{1,0:T(4,128)S(1)}, f32[4,128]{1,0:T(4,128)}, u32[]{:S(2)}) copy-start(f32[4,128]{1,0:T(4,128)} %param.10) | copy-start | bytes 6148
  44.9 2.4 %copy-start.6 = (f32[4,256,256]{1,2,0:T(8,128)S(1)}, f32[4,256,256]{1,2,0:T(8,128)}, u32[]{:S(2)}) copy-start(f32[4,256,256]{1,2,0:T(8,128)} %get-tuple-element.65) | copy-start | bytes 3145732
  44.9 2.4 %copy-start.17 = (pred[256,256]{0,1:T(8,128)(4,1)S(1)}, pred[256,256]{0,1:T(8,128)(4,1)}, u32[]{:S(2)}) copy-start(pred[256,256]{0,1:T(8,128)(4,1)} %copy-done.16) | copy-start | bytes 196612
  44.9 2.4 %copy-start.19 = (pred[256,256]{0,1:T(8,128)(4,1)S(1)}, pred[256,256]{0,1:T(8,128)(4,1)}, u32[]{:S(2)}) copy-start(pred[256,256]{0,1:T(8,128)(4,1)} %copy-done.18) | copy-start | bytes 196612
  44.9 2.4 %copy-start.21 = (pred[256,256]{0,1:T(8,128)(4,1)S(1)}, pred[256,256]{0,1:T(8,128)(4,1)}, u32[]{:S(2)}) copy-start(pred[256,256]{0,1:T(8,128)(4,1)} %copy-done.20) | copy-start | bytes 196612
  44.9 2.4 %copy-start.23 = (pred[256,256]{0,1:T(8,128)(4,1)S(1)}, pred[256,256]{0,1:T(8,128)(4,1)}, u32[]{:S(2)}) copy-start(pred[256,256]{0,1:T(8,128)(4,1)} %copy-done.22) | copy-start | bytes 196612
  45.0 2.4 %copy-start.25 = (pred[256,256]{0,1:T(8,128)(4,1)S(1)}, pred[256,256]{0,1:T(8,128)(4,1)}, u32[]{:S(2)}) copy-start(pred[256,256]{0,1:T(8,128)(4,1)} %copy-done.24) | copy-start | bytes 196612
  45.0 2.4 %copy-start.27 = (pred[256,256]{0,1:T(8,128)(4,1)S(1)}, pred[256,256]{0,1:T(8,128)(4,1)}, u32[]{:S(2)}) copy-start(pred[256,256]{0,1:T(8,128)(4,1)} %copy-done.26) | copy-start | bytes 196612
  45.0 2.4 %copy-start.29 = (pred[256,256]{0,1:T(8,128)(4,1)S(1)}, pred[256,256]{0,1:T(8,128)(4,1)}, u32[]{:S(2)}) copy-start(pred[256,256]{0,1:T(8,128)(4,1)} %copy-done.28) | copy-start | bytes 196612
  47.3 1.0 %copy-start.3 = (f32[4,256,128]{1,2,0:T(8,128)S(1)}, f32[4,256,128]{1,2,0:T(8,128)}, u32[]{:S(2)}) copy-start(f32[4,256,128]{1,2,0:T(8,128)} %copy.42) | copy-start | bytes 1572868
  48.8 5.1 %copy-start.5 = (bf16[4,256,256]{1,2,0:T(8,128)(2,1)S(1)}, bf16[4,256,256]{1,2,0:T(8,128)(2,1)}, u32[]{:S(2)}) copy-start(bf16[4,256,256]{1,2,0:T(8,128)(2,1)} %copy-done.4) | copy-start | bytes 1572868
  49.5 1.5 %collective-permute-start.10 = (f32[4,128,128]{2,1,0:T(8,128)S(1)}, f32[4,128,128]{2,1,0:T(8,128)S(1)}, u32[]{:S(2)}, u32[]{:S(2)}) collective-permute-start(f32[4,128,128]{2,1,0:T(8,128)S(1)} %get-tuple-element.34), channel_id=1, source_target_pairs={{0,1},{1,0},{2,3},{3,2},{4,5},{5,4},{6,7},{7,6},{8,9},{9,8},{10,11... | collective-permute-start | bytes 786440 | tf_op jit(solution)/shard_map/ppermute | solution.py:14
  49.6 1.9 %collective-permute-start.5 = (f32[4,128,128]{2,1,0:T(8,128)S(1)}, f32[4,128,128]{2,1,0:T(8,128)S(1)}, u32[]{:S(2)}, u32[]{:S(2)}) collective-permute-start(f32[4,128,128]{2,1,0:T(8,128)S(1)} %get-tuple-element.36), channel_id=1, source_target_pairs={{0,1},{1,0},{2,3},{3,2},{4,5},{5,4},{6,7},{7,6},{8,9},{9,8},{10,11... | collective-permute-start | bytes 786440 | tf_op jit(solution)/shard_map/ppermute | solution.py:14
  50.1 1.8 %collective-permute-start.7 = (f32[4,128,128]{2,1,0:T(8,128)S(1)}, f32[4,128,128]{2,1,0:T(8,128)S(1)}, u32[]{:S(2)}, u32[]{:S(2)}) collective-permute-start(f32[4,128,128]{2,1,0:T(8,128)S(1)} %get-tuple-element.35), channel_id=1, source_target_pairs={{0,1},{1,0},{2,3},{3,2},{4,5},{5,4},{6,7},{7,6},{8,9},{9,8},{10,11... | collective-permute-start | bytes 786440 | tf_op jit(solution)/shard_map/ppermute | solution.py:14
  50.1 24.6 %collective-permute-start.4 = (f32[4,128,128]{2,1,0:T(8,128)}, f32[4,128,128]{2,1,0:T(8,128)}, u32[]{:S(2)}, u32[]{:S(2)}) collective-permute-start(f32[4,128,128]{2,1,0:T(8,128)} %get-tuple-element.33), channel_id=1, source_target_pairs={{0,1},{1,0},{2,3},{3,2},{4,5},{5,4},{6,7},{7,6},{8,9},{9,8},{10,11... | collective-permute-start | bytes 786440 | tf_op jit(solution)/shard_map/ppermute | solution.py:14
  50.7 11.6 %copy-start.8 = (f32[1,4,128,128]{3,2,1,0:T(8,128)S(1)}, f32[1,4,128,128]{3,2,1,0:T(8,128)}, u32[]{:S(2)}) copy-start(f32[1,4,128,128]{3,2,1,0:T(8,128)} %copy-done.7) | copy-start | bytes 786436
  50.7 11.6 %copy-start.10 = (f32[1,4,128,128]{3,2,1,0:T(8,128)S(1)}, f32[1,4,128,128]{3,2,1,0:T(8,128)}, u32[]{:S(2)}) copy-start(f32[1,4,128,128]{3,2,1,0:T(8,128)} %copy-done.9) | copy-start | bytes 786436
  50.7 11.6 %copy-start.12 = (f32[1,4,128,128]{3,2,1,0:T(8,128)S(1)}, f32[1,4,128,128]{3,2,1,0:T(8,128)}, u32[]{:S(2)}) copy-start(f32[1,4,128,128]{3,2,1,0:T(8,128)} %get-tuple-element.43) | copy-start | bytes 786436
  50.7 11.6 %copy-start.14 = (f32[1,4,128,128]{3,2,1,0:T(8,128)S(1)}, f32[1,4,128,128]{3,2,1,0:T(8,128)}, u32[]{:S(2)}) copy-start(f32[1,4,128,128]{3,2,1,0:T(8,128)} %copy-done.13) | copy-start | bytes 786436
  52.6 9.2 %collective-permute-start.11 = (f32[4,128,128]{2,1,0:T(8,128)S(1)}, f32[4,128,128]{2,1,0:T(8,128)S(1)}, u32[]{:S(2)}, u32[]{:S(2)}) collective-permute-start(f32[4,128,128]{2,1,0:T(8,128)S(1)} %get-tuple-element.38), channel_id=1, source_target_pairs={{0,2},{1,3},{2,0},{3,1},{4,6},{5,7},{6,4},{7,5},{8,10},{9,11},{10,... | collective-permute-start | bytes 786440 | tf_op jit(solution)/shard_map/ppermute | solution.py:14
  53.8 10.3 %copy-start.42 = (f32[4,13,256]{2,0,1:T(4,128)}, f32[4,13,256]{2,0,1:T(4,128)S(1)}, u32[]{:S(2)}) copy-start(f32[4,13,256]{2,0,1:T(4,128)S(1)} %constant_dynamic-update-slice_fusion) | copy-start | bytes 159748
  54.1 14.0 %collective-permute-start.8 = (f32[4,128,128]{2,1,0:T(8,128)S(1)}, f32[4,128,128]{2,1,0:T(8,128)}, u32[]{:S(2)}, u32[]{:S(2)}) collective-permute-start(f32[4,128,128]{2,1,0:T(8,128)S(1)} %get-tuple-element.39), channel_id=1, source_target_pairs={{0,2},{1,3},{2,0},{3,1},{4,6},{5,7},{6,4},{7,5},{8,10},{9,11},{10,... | collective-permute-start | bytes 786440 | tf_op jit(solution)/shard_map/ppermute | solution.py:14
  61.8 8.7 %collective-permute-start.12 = (f32[4,128,128]{2,1,0:T(8,128)S(1)}, f32[4,128,128]{2,1,0:T(8,128)}, u32[]{:S(2)}, u32[]{:S(2)}) collective-permute-start(f32[4,128,128]{2,1,0:T(8,128)S(1)} %add.369), channel_id=1, source_target_pairs={{0,4},{1,5},{2,6},{3,7},{4,0},{5,1},{6,2},{7,3},{8,12},{9,13},{10,... | collective-permute-start | bytes 786440 | tf_op jit(solution)/shard_map/ppermute | solution.py:14
  64.1 2.4 %copy-start.15 = (f32[4,128,128]{2,1,0:T(8,128)S(1)}, f32[4,128,128]{2,1,0:T(8,128)}, u32[]{:S(2)}) copy-start(f32[4,128,128]{2,1,0:T(8,128)} %get-tuple-element.37) | copy-start | bytes 786436
  66.6 8.1 %collective-permute-start.6 = (f32[4,128,128]{2,1,0:T(8,128)S(1)}, f32[4,128,128]{2,1,0:T(8,128)S(1)}, u32[]{:S(2)}, u32[]{:S(2)}) collective-permute-start(f32[4,128,128]{2,1,0:T(8,128)S(1)} %copy-done.15), channel_id=1, source_target_pairs={{0,2},{1,3},{2,0},{3,1},{4,6},{5,7},{6,4},{7,5},{8,10},{9,11},{10,... | collective-permute-start | bytes 786440 | tf_op jit(solution)/shard_map/ppermute | solution.py:14
  69.1 11.4 %collective-permute-start.9 = (f32[4,128,128]{2,1,0:T(8,128)S(1)}, f32[4,128,128]{2,1,0:T(8,128)S(1)}, u32[]{:S(2)}, u32[]{:S(2)}) collective-permute-start(f32[4,128,128]{2,1,0:T(8,128)S(1)} %add.366), channel_id=1, source_target_pairs={{0,4},{1,5},{2,6},{3,7},{4,0},{5,1},{6,2},{7,3},{8,12},{9,13},{10,... | collective-permute-start | bytes 786440 | tf_op jit(solution)/shard_map/ppermute | solution.py:14
  71.5 12.4 %collective-permute-start.13 = (f32[4,128,128]{2,1,0:T(8,128)S(1)}, f32[4,128,128]{2,1,0:T(8,128)S(1)}, u32[]{:S(2)}, u32[]{:S(2)}) collective-permute-start(f32[4,128,128]{2,1,0:T(8,128)S(1)} %add.370), channel_id=1, source_target_pairs={{0,8},{1,9},{2,10},{3,11},{4,12},{5,13},{6,14},{7,15},{8,0},{9,1},... | collective-permute-start | bytes 786440 | tf_op jit(solution)/shard_map/ppermute | solution.py:14
where the time goes:
time: 87.2 us; the launch traced here: 86.8 us
  waiting for transfers between devices  37.5 us (43%)
  starting transfers between devices  16.6 us (19%)
  matrix products  13.5 us (15%)
  other arithmetic  7.87 us (9%)
  local copies, waits for them, and re-layouts  5.16 us (6%)
  blocking collectives  4.91 us (6%)
  between operations  1.32 us (2%)
    ppermute x14, waiting for transfers between devices, from_partner(): return lax.ppermute(value, axis, pairs)  37.5 us
    ppermute x14, starting transfers between devices, from_partner(): return lax.ppermute(value, axis, pairs)  16.6 us
    psum x1, blocking collectives, shards(): totals = lax.psum(jnp.sum(attended * attended, axis=(0, 2)), 'heads')  4.91 us
    add x4, other arithmetic, shards(): level_total = level_total + partner  2.78 us
    dot_general x1, matrix products, shards(): jnp.einsum('hte,hse->hts', grad_out, value_rows, preferred_element_type=j...  2.28 us
    unnamed x88, local copies, waits for them, and re-layouts  2.15 us
    dot_general x1, matrix products, shards(): jnp.einsum('htd,hsd->hts', queries, key_rows, preferred_element_type=jnp....  2.01 us
    dot_general x1, matrix products, shards(): jnp.einsum('hte,mhde->mhtd', grad_wide, states, precision=HIGH)  1.84 us
  transfers between devices with their start and end apart: 14, of which 10 were waited for; matrix products, arithmetic and copies ran while one was open for 14% of the time, Pallas kernels for 0%

commit v1 on v0

--- a/solution.py
+++ b/solution.py
@@ -74,7 +74,7 @@
     query_wide = queries.astype(jnp.float32)
     far_terms = jnp.einsum("htd,mhde->mhte", query_wide, states, precision=HIGH)
     attended = near_out + jnp.sum(far_scale[..., None] * far_terms, 0)
-    totals = lax.psum(jnp.sum(attended * attended, axis=(0, 2)), "heads")
+    totals = jnp.sum(lax.all_gather(jnp.sum(attended * attended, axis=(0, 2)), "heads"), axis=0)
     inv_rms = lax.rsqrt(totals / width + EPS)
     normed = (attended * inv_rms[None, :, None] * norm_gain[:, None, :]).astype(jnp.bfloat16)
     scaled = norm_gain[:, None, :] * grad_normed.astype(jnp.float32)

time: 87.2 us -> 91.5 us (1.049)
  blocking collectives: 4.91 us -> 9.14 us
    all_gather x0 -> x1, blocking collectives: none -> 4.23 us  [shards(): lax.all_gather(jnp.sum(attended * attended, axis=(0, 2)), 'heads')]
where the time goes in v1:
time: 91.5 us; the launch traced here: 91.1 us
  waiting for transfers between devices  37.5 us (41%)
  starting transfers between devices  16.5 us (18%)
  matrix products  13.6 us (15%)
  blocking collectives  9.14 us (10%)
  other arithmetic  7.91 us (9%)
  local copies, waits for them, and re-layouts  5.18 us (6%)
  between operations  1.33 us (1%)
    ppermute x14, waiting for transfers between devices, from_partner(): return lax.ppermute(value, axis, pairs)  37.5 us
    ppermute x14, starting transfers between devices, from_partner(): return lax.ppermute(value, axis, pairs)  16.5 us
    psum x1, blocking collectives, shards(): inner_sum = lax.psum(jnp.sum(scaled * attended, axis=(0, 2)), 'heads')  4.91 us
    all_gather x1, blocking collectives, shards(): lax.all_gather(jnp.sum(attended * attended, axis=(0, 2)), 'heads')  4.23 us
    add x4, other arithmetic, shards(): level_total = level_total + partner  2.8 us
    dot_general x1, matrix products, shards(): jnp.einsum('hte,hse->hts', grad_out, value_rows, preferred_element_type=j...  2.29 us
    unnamed x88, local copies, waits for them, and re-layouts  2.15 us
    dot_general x1, matrix products, shards(): jnp.einsum('htd,hsd->hts', queries, key_rows, preferred_element_type=jnp....  2.01 us
  transfers between devices with their start and end apart: 14, of which 10 were waited for; matrix products, arithmetic and copies ran while one was open for 14% of the time, Pallas kernels for 0%

profile of v1, /device:TPU:0, one launch (start us, length us, event | category | flops | bytes accessed | tf_op | source)
XLA Modules:
  0.0 91.1 jit_solution(14427903694990783664)
XLA Ops:
  0.6 0.0 copy-start
  0.7 0.9 %copy-done = bf16[4,256,128]{2,1,0:T(8,128)(2,1)S(1)} copy-done((bf16[4,256,128]{2,1,0:T(8,128)(2,1)S(1)}, bf16[4,256,128]{2,1,0:T(8,128)(2,1)}, u32[]{:S(2)}) %copy-start) | copy-done | bytes 262168
  1.6 1.2 %fusion.39 = f32[4,128,128]{2,1,0:T(8,128)S(1)} fusion(bf16[4,256,128]{2,1,0:T(8,128)(2,1)} %param.7, bf16[4,256,128]{2,1,0:T(8,128)(2,1)S(1)} %copy-done), kind=kOutput, calls=%fused_computation.115 | convolution fusion | flops 33554432 | bytes 786432 | tf_op jit(solution)/shard_map/hsd,hse->hde/dot_general | solution.py:51
  2.8 0.6 collective-permute-start
  3.4 0.2 fusion.20
  3.5 0.2 fusion.22
  3.7 0.8 collective-permute-done
  4.6 0.0 copy-start.9
  4.6 0.0 copy-start.1
  4.6 2.9 %collective-permute-start.1 = (f32[4,128,128]{2,1,0:T(8,128)S(1)}, f32[4,128,128]{2,1,0:T(8,128)S(1)}, u32[]{:S(2)}, u32[]{:S(2)}) collective-permute-start(f32[4,128,128]{2,1,0:T(8,128)S(1)} %get-tuple-element.40), channel_id=1, source_target_pairs={{0,2},{1,3},{2,0},{3,1},{4,6},{5,7},{6,4},{7,5},{8,10},{9,11},{10,... | collective-permute-start | bytes 786440 | tf_op jit(solution)/shard_map/ppermute | solution.py:14
  7.5 0.1 fusion.28
  7.7 0.0 copy-start.34
  7.8 6.3 %collective-permute-done.1 = f32[4,128,128]{2,1,0:T(8,128)S(1)} collective-permute-done((f32[4,128,128]{2,1,0:T(8,128)S(1)}, f32[4,128,128]{2,1,0:T(8,128)S(1)}, u32[]{:S(2)}, u32[]{:S(2)}) %collective-permute-start.1) | collective-permute-done | bytes 262176 | tf_op jit(solution)/shard_map/ppermute | solution.py:14
  14.1 0.7 select_bitcast_fusion.2
  14.9 1.8 %collective-permute-start.2 = (f32[4,128,128]{2,1,0:T(8,128)S(1)}, f32[4,128,128]{2,1,0:T(8,128)S(1)}, u32[]{:S(2)}, u32[]{:S(2)}) collective-permute-start(f32[4,128,128]{2,1,0:T(8,128)S(1)} %get-tuple-element.42), channel_id=1, source_target_pairs={{0,4},{1,5},{2,6},{3,7},{4,0},{5,1},{6,2},{7,3},{8,12},{9,13},{10,... | collective-permute-start | bytes 786440 | tf_op jit(solution)/shard_map/ppermute | solution.py:14
  16.7 0.1 copy.35
  16.9 1.0 %copy.42 = f32[4,256,128]{1,2,0:T(8,128)} copy(bf16[4,256,128]{2,1,0:T(8,128)(2,1)S(1)} %copy-done.2) | data formatting | bytes 786432 | tf_op jit(solution)/shard_map/convert_element_type | solution.py:102
  17.8 0.2 fusion.24
  18.0 0.2 fusion.26
  18.2 4.4 %collective-permute-done.2 = f32[4,128,128]{2,1,0:T(8,128)S(1)} collective-permute-done((f32[4,128,128]{2,1,0:T(8,128)S(1)}, f32[4,128,128]{2,1,0:T(8,128)S(1)}, u32[]{:S(2)}, u32[]{:S(2)}) %collective-permute-start.2) | collective-permute-done | bytes 262176 | tf_op jit(solution)/shard_map/ppermute | solution.py:14
  22.7 0.0 copy-start.13
  22.7 2.6 %collective-permute-start.3 = (f32[4,128,128]{2,1,0:T(8,128)S(1)}, f32[4,128,128]{2,1,0:T(8,128)S(1)}, u32[]{:S(2)}, u32[]{:S(2)}) collective-permute-start(f32[4,128,128]{2,1,0:T(8,128)S(1)} %get-tuple-element.44), channel_id=1, source_target_pairs={{0,8},{1,9},{2,10},{3,11},{4,12},{5,13},{6,14},{7,15},{8,0},{9,1},... | collective-permute-start | bytes 786440 | tf_op jit(solution)/shard_map/ppermute | solution.py:14
  25.3 2.0 %multiply_convert_fusion.3 = (bf16[4,256,256]{1,2,0:T(8,128)(2,1)S(1)}, f32[4,256,256]{1,2,0:T(8,128)}) fusion(f32[4,256]{1,0:T(4,128)S(1)} %get-tuple-element.48, pred[256,256]{0,1:T(8,128)(4,1)S(1)} %get-tuple-element.67, f32[4,256]{1,0:T(4,128)S(1)} %get-tuple-element.49, pred[256,256]{0,1:T(8,128)(4,1)S(1)} %get-tuple-element.68, ...), kind=kOutput, calls=%fused_computation.28 | convolution fusion | flops 72089600 | bytes 2723840 | tf_op jit(solution)/shard_map/htd,hsd->hts/dot_general | solution.py:64
  27.5 8.7 %collective-permute-done.3 = f32[4,128,128]{2,1,0:T(8,128)S(1)} collective-permute-done((f32[4,128,128]{2,1,0:T(8,128)S(1)}, f32[4,128,128]{2,1,0:T(8,128)S(1)}, u32[]{:S(2)}, u32[]{:S(2)}) %collective-permute-start.3) | collective-permute-done | bytes 262176 | tf_op jit(solution)/shard_map/ppermute | solution.py:14
  36.2 0.0 copy-start.7
  36.2 0.0 copy-start.32
  36.3 1.1 %multiply_reduce_fusion = (f32[4,256,128]{1,2,0:T(8,128)S(1)}, f32[4,4,256,128]{2,3,1,0:T(8,128)S(1)}) fusion(f32[4,4,256]{2,1,0:T(4,128)S(1)} %pad_maximum_fusion.3, bf16[4,256,128]{2,1,0:T(8,128)(2,1)S(1)} %copy-done.2, f32[1,4,128,128]{3,2,1,0:T(8,128)S(1)} %select_bitcast_fusion, f32[1,4,128,128]{3,2,1,0:T(8,128)S(1)} %get-tuple-element.43, ...), kind=kOutput, calls=%fused_computation.3 | convolution fusion | flops 807010304 | bytes 3948544 | tf_op jit(solution)/shard_map/htd,mhde->mhte/dot_general | solution.py:75
  37.4 1.1 %multiply_reduce_fusion.1 = (f32[256]{0:T(256)S(1)}, f32[256]{0:T(256)S(1)}, f32[4,256,128]{1,2,0:T(8,128)}) fusion(bf16[4,256,128]{1,2,0:T(8,128)(2,1)S(1)} %copy.35, f32[4,128]{1,0:T(4,128)S(1)} %copy-done.32, f32[4,256,128]{1,2,0:T(8,128)S(1)} %get-tuple-element.60, bf16[4,256,256]{1,2,0:T(8,128)(2,1)S(1)} %get-tuple-element.62, ...), kind=kOutput, calls=%fused_computation.43 | convolution fusion | flops 68025856 | bytes 2101248 | tf_op jit(solution)/shard_map/hts,hse->hte/dot_general | solution.py:66
  38.6 4.2 %all-gather.1 = f32[2,1,256]{2,1,0:T(1,128)S(1)} all-gather(f32[1,1,256]{2,1,0:T(1,128)S(1)} %bitcast.140), channel_id=2, replica_groups=mesh['heads'=2,'ctx'=16] {'heads'}, dimensions={0}, use_global_device_ids=true | all-gather | bytes 3072 | tf_op jit(solution)/shard_map/all_gather | solution.py:77
  42.8 4.9 %psum.7 = f32[256]{0:T(256)S(1)} all-reduce(f32[256]{0:T(256)S(1)} %get-tuple-element.28), channel_id=1, replica_groups=mesh['heads'=2,'ctx'=16] {'heads'}, use_global_device_ids=true, to_apply=%region_4.5 | all-reduce | flops 256 | bytes 2048 | tf_op jit(solution)/shard_map/psum | solution.py:81
  47.8 1.4 %fusion.11 = (f32[4,256]{1,0:T(4,128)S(1)}, f32[4,256]{1,0:T(4,128)S(1)}, f32[4,256]{1,0:T(4,128)S(1)}, f32[4,256]{1,0:T(4,128)S(1)}, bf16[4,256,128]{1,2,0:T(8,128)(2,1)S(1)}, /*index=5*/bf16[4,256,128]{1,2,0:T(8,128)(2,1)S(1)}) fusion(f32[4,4,256,128]{2,3,1,0:T(8,128)S(1)} %get-tuple-element.61, f32[4,256,128]{1,2,0:T(8,128)} %get-tuple-element.64, ...), kind=kLoop, calls=%fused_computation.37 | loop fusion | flops 2355200 | bytes 3428352 | tf_op jit(solution)/shard_map/reduce_sum | solution.py:94
  49.3 2.3 %multiply_convert_fusion.2 = (bf16[4,256,256]{1,2,0:T(8,128)(2,1)S(1)}, f32[4,256,256]{1,2,0:T(8,128)S(1)}) fusion(f32[4,256]{1,0:T(4,128)} %copy-done.34, pred[256,256]{0,1:T(8,128)(4,1)S(1)} %get-tuple-element.67, f32[4,256]{1,0:T(4,128)} %copy-done.35, pred[256,256]{0,1:T(8,128)(4,1)S(1)} %get-tuple-element.68, f32[4,256]{1,0:T(4,128)} %copy-done.36, ...), kind=kOutput, calls=%fused_computation.26 | convolution fusion | flops 72089600 | bytes 2723840 | tf_op jit(solution)/shard_map/hte,hse->hts/dot_general | solution.py:86
  51.6 0.9 select_reduce_fusion
  52.6 0.0 copy-done.3
  52.6 0.4 convolution_bitcast_fusion.1
  53.0 0.8 slice_bitcast_fusion.7
  53.8 0.5 collective-permute-start.5
  54.3 0.5 collective-permute-start.4
  55.0 0.0 copy-start.8
  55.0 0.0 copy-start.14
  55.0 0.4 collective-permute-done.10
  55.4 0.4 collective-permute-done.5
  55.7 0.4 collective-permute-done.7
  56.1 0.8 fusion.36
  56.9 1.2 %collective-permute-start.11 = (f32[4,128,128]{2,1,0:T(8,128)S(1)}, f32[4,128,128]{2,1,0:T(8,128)S(1)}, u32[]{:S(2)}, u32[]{:S(2)}) collective-permute-start(f32[4,128,128]{2,1,0:T(8,128)S(1)} %get-tuple-element.36), channel_id=1, source_target_pairs={{0,2},{1,3},{2,0},{3,1},{4,6},{5,7},{6,4},{7,5},{8,10},{9,11},{10,... | collective-permute-start | bytes 786440 | tf_op jit(solution)/shard_map/ppermute | solution.py:14
  58.1 0.3 fusion.41
  58.4 0.9 %collective-permute-start.8 = (f32[4,128,128]{2,1,0:T(8,128)S(1)}, f32[4,128,128]{2,1,0:T(8,128)}, u32[]{:S(2)}, u32[]{:S(2)}) collective-permute-start(f32[4,128,128]{2,1,0:T(8,128)S(1)} %get-tuple-element.37), channel_id=1, source_target_pairs={{0,2},{1,3},{2,0},{3,1},{4,6},{5,7},{6,4},{7,5},{8,10},{9,11},{10,... | collective-permute-start | bytes 786440 | tf_op jit(solution)/shard_map/ppermute | solution.py:14
  59.3 6.8 %collective-permute-done.11 = f32[4,128,128]{2,1,0:T(8,128)S(1)} collective-permute-done((f32[4,128,128]{2,1,0:T(8,128)S(1)}, f32[4,128,128]{2,1,0:T(8,128)S(1)}, u32[]{:S(2)}, u32[]{:S(2)}) %collective-permute-start.11) | collective-permute-done | bytes 262176 | tf_op jit(solution)/shard_map/ppermute | solution.py:14
  66.1 0.4 collective-permute-start.12
  66.6 1.8 %fusion = f32[4,256,128]{1,2,0:T(8,128)} fusion(f32[4,4,256]{2,1,0:T(4,128)S(1)} %pad_maximum_fusion.3, f32[1,4,128,128]{3,2,1,0:T(8,128)S(1)} %copy-done.8, f32[1,4,128,128]{3,2,1,0:T(8,128)S(1)} %copy-done.14, f32[1,4,128,128]{3,2,1,0:T(8,128)S(1)} %copy-done.12, f32[1,4,128,128]{3,2,1,0:T(8,128)S(1)} %copy-done.10, ...), kind=kOutput, calls=%fused_computation.1 | convolution fusion | flops 807010304 | bytes 1851392 | tf_op jit(solution)/shard_map/hte,mhde->mhtd/dot_general | solution.py:100
  68.4 1.3 %copy.41 = f32[4,256,128]{2,1,0:T(8,128)S(1)} copy(f32[4,256,128]{1,2,0:T(8,128)} %fusion) | data formatting | bytes 1048576 | tf_op jit(solution)/shard_map/reduce_sum | solution.py:99
  69.7 0.8 copy.49
  70.5 0.3 fusion.40
  70.8 1.6 %collective-permute-start.6 = (f32[4,128,128]{2,1,0:T(8,128)S(1)}, f32[4,128,128]{2,1,0:T(8,128)S(1)}, u32[]{:S(2)}, u32[]{:S(2)}) collective-permute-start(f32[4,128,128]{2,1,0:T(8,128)S(1)} %copy-done.15), channel_id=1, source_target_pairs={{0,2},{1,3},{2,0},{3,1},{4,6},{5,7},{6,4},{7,5},{8,10},{9,11},{10,... | collective-permute-start | bytes 786440 | tf_op jit(solution)/shard_map/ppermute | solution.py:14
  72.4 1.0 %add.368 = f32[4,128,128]{2,1,0:T(8,128)S(1)} add(f32[4,128,128]{2,1,0:T(8,128)S(1)} %get-tuple-element.37, f32[4,128,128]{2,1,0:T(8,128)} %collective-permute-done.8) | non-fusion elementwise | flops 65536 | bytes 786432 | tf_op jit(solution)/shard_map/add | solution.py:112
  73.4 1.4 %collective-permute-start.9 = (f32[4,128,128]{2,1,0:T(8,128)S(1)}, f32[4,128,128]{2,1,0:T(8,128)S(1)}, u32[]{:S(2)}, u32[]{:S(2)}) collective-permute-start(f32[4,128,128]{2,1,0:T(8,128)S(1)} %add.368), channel_id=1, source_target_pairs={{0,4},{1,5},{2,6},{3,7},{4,0},{5,1},{6,2},{7,3},{8,12},{9,13},{10,... | collective-permute-start | bytes 786440 | tf_op jit(solution)/shard_map/ppermute | solution.py:14
  74.8 1.0 %add.372 = f32[4,128,128]{2,1,0:T(8,128)S(1)} add(f32[4,128,128]{2,1,0:T(8,128)S(1)} %add.371, f32[4,128,128]{2,1,0:T(8,128)} %collective-permute-done.12) | non-fusion elementwise | flops 65536 | bytes 786432 | tf_op jit(solution)/shard_map/add | solution.py:112
  75.8 2.1 %collective-permute-start.13 = (f32[4,128,128]{2,1,0:T(8,128)S(1)}, f32[4,128,128]{2,1,0:T(8,128)S(1)}, u32[]{:S(2)}, u32[]{:S(2)}) collective-permute-start(f32[4,128,128]{2,1,0:T(8,128)S(1)} %add.372), channel_id=1, source_target_pairs={{0,8},{1,9},{2,10},{3,11},{4,12},{5,13},{6,14},{7,15},{8,0},{9,1},... | collective-permute-start | bytes 786440 | tf_op jit(solution)/shard_map/ppermute | solution.py:14
  77.9 1.1 %fusion.3 = bf16[4,256,128]{2,1,0:T(8,128)(2,1)} fusion(f32[4,256,128]{2,1,0:T(8,128)S(1)} %copy.41, bf16[4,256,256]{1,2,0:T(8,128)(2,1)S(1)} %get-tuple-element.65, bf16[4,256,128]{2,1,0:T(8,128)(2,1)S(1)} %copy-done.1), kind=kOutput, calls=%fused_computation.12 | convolution fusion | flops 67371008 | bytes 1572864 | tf_op jit(solution)/shard_map/hts,hsd->htd/dot_general | solution.py:98
  79.0 5.8 %collective-permute-done.9 = f32[4,128,128]{2,1,0:T(8,128)S(1)} collective-permute-done((f32[4,128,128]{2,1,0:T(8,128)S(1)}, f32[4,128,128]{2,1,0:T(8,128)S(1)}, u32[]{:S(2)}, u32[]{:S(2)}) %collective-permute-start.9) | collective-permute-done | bytes 262176 | tf_op jit(solution)/shard_map/ppermute | solution.py:14
  84.8 3.4 %collective-permute-done.13 = f32[4,128,128]{2,1,0:T(8,128)S(1)} collective-permute-done((f32[4,128,128]{2,1,0:T(8,128)S(1)}, f32[4,128,128]{2,1,0:T(8,128)S(1)}, u32[]{:S(2)}, u32[]{:S(2)}) %collective-permute-start.13) | collective-permute-done | bytes 262176 | tf_op jit(solution)/shard_map/ppermute | solution.py:14
  88.2 1.0 %add_convert_fusion = bf16[4,128,128]{2,1,0:T(8,128)(2,1)S(1)} fusion(f32[4,128,128]{2,1,0:T(8,128)S(1)} %collective-permute-done.13, f32[4,128,128]{2,1,0:T(8,128)S(1)} %collective-permute-done.9, f32[4,128,128]{2,1,0:T(8,128)S(1)} %collective-permute-done.6, f32[4,128,128]{2,1,0:T(8,128)} %collective-permute-done.4, pred[]{:T(512)S(6)} %eq.94, ...), kind=kLoop, calls=%fused_computation.73 | loop fusion | flops 524288 | bytes 1179652 | tf_op jit(solution)/shard_map/convert_element_type | solution.py:116
  89.2 0.9 %fusion.4 = bf16[4,256,128]{2,1,0:T(8,128)(2,1)} fusion(f32[4,256,128]{2,1,0:T(8,128)S(1)} %fusion.41, bf16[4,256,128]{2,1,0:T(8,128)(2,1)S(1)} %copy-done.1, bf16[4,128,128]{2,1,0:T(8,128)(2,1)S(1)} %add_convert_fusion), kind=kOutput, calls=%fused_computation.13 | convolution fusion | flops 33816576 | bytes 1179648 | tf_op jit(solution)/shard_map/hsd,hde->hse/dot_general | solution.py:122
  90.2 0.9 %fusion.5 = bf16[4,256,128]{2,1,0:T(8,128)(2,1)} fusion(f32[4,256,128]{2,1,0:T(8,128)S(1)} %fusion.40, bf16[4,128,128]{2,1,0:T(8,128)(2,1)S(1)} %add_convert_fusion, bf16[4,256,128]{2,1,0:T(8,128)(2,1)S(1)} %copy-done), kind=kOutput, calls=%fused_computation.14 | convolution fusion | flops 33816576 | bytes 1179648 | tf_op jit(solution)/shard_map/hse,hde->hsd/dot_general | solution.py:118
  (102 shorter events, 0.5 us)
Async XLA Ops:
  0.6 1.0 %copy-start = (bf16[4,256,128]{2,1,0:T(8,128)(2,1)S(1)}, bf16[4,256,128]{2,1,0:T(8,128)(2,1)}, u32[]{:S(2)}) copy-start(bf16[4,256,128]{2,1,0:T(8,128)(2,1)} %param.8) | copy-start | bytes 786436
  0.6 7.0 %copy-start.31 = (f32[4,13,256]{2,0,1:T(4,128)S(1)}, f32[4,13,256]{2,0,1:T(4,128)}, u32[]{:S(2)}) copy-start(f32[4,13,256]{2,0,1:T(4,128)} %param.9) | copy-start | bytes 159748
  0.7 16.0 %copy-start.30 = (bf16[4,256,128]{2,1,0:T(8,128)(2,1)S(1)}, bf16[4,256,128]{2,1,0:T(8,128)(2,1)}, u32[]{:S(2)}) copy-start(bf16[4,256,128]{2,1,0:T(8,128)(2,1)} %param.11) | copy-start | bytes 786436
  0.7 16.2 %copy-start.2 = (bf16[4,256,128]{2,1,0:T(8,128)(2,1)S(1)}, bf16[4,256,128]{2,1,0:T(8,128)(2,1)}, u32[]{:S(2)}) copy-start(bf16[4,256,128]{2,1,0:T(8,128)(2,1)} %param.6) | copy-start | bytes 786436
  2.8 1.7 %collective-permute-start = (f32[4,128,128]{2,1,0:T(8,128)S(1)}, f32[4,128,128]{2,1,0:T(8,128)S(1)}, u32[]{:S(2)}, u32[]{:S(2)}) collective-permute-start(f32[4,128,128]{2,1,0:T(8,128)S(1)} %fusion.39), channel_id=1, source_target_pairs={{0,1},{1,0},{2,3},{3,2},{4,5},{5,4},{6,7},{7,6},{8,9},{9,8},{10,11... | collective-permute-start | bytes 786440 | tf_op jit(solution)/shard_map/ppermute | solution.py:14
  3.7 23.6 %copy-start.16 = (pred[256,256]{0,1:T(8,128)(4,1)}, pred[256,256]{0,1:T(8,128)(4,1)S(1)}, u32[]{:S(2)}) copy-start(pred[256,256]{0,1:T(8,128)(4,1)S(1)} %get-tuple-element.69) | copy-start | bytes 196612
  3.7 23.6 %copy-start.18 = (pred[256,256]{0,1:T(8,128)(4,1)}, pred[256,256]{0,1:T(8,128)(4,1)S(1)}, u32[]{:S(2)}) copy-start(pred[256,256]{0,1:T(8,128)(4,1)S(1)} %get-tuple-element.70) | copy-start | bytes 196612
  4.6 31.7 %copy-start.9 = (f32[1,4,128,128]{3,2,1,0:T(8,128)}, f32[1,4,128,128]{3,2,1,0:T(8,128)S(1)}, u32[]{:S(2)}) copy-start(f32[1,4,128,128]{3,2,1,0:T(8,128)S(1)} %get-tuple-element.39) | copy-start | bytes 786436
  4.6 20.7 %copy-start.1 = (bf16[4,256,128]{2,1,0:T(8,128)(2,1)S(1)}, bf16[4,256,128]{2,1,0:T(8,128)(2,1)}, u32[]{:S(2)}) copy-start(bf16[4,256,128]{2,1,0:T(8,128)(2,1)} %param.7) | copy-start | bytes 786436
  4.6 9.5 %collective-permute-start.1 = (f32[4,128,128]{2,1,0:T(8,128)S(1)}, f32[4,128,128]{2,1,0:T(8,128)S(1)}, u32[]{:S(2)}, u32[]{:S(2)}) collective-permute-start(f32[4,128,128]{2,1,0:T(8,128)S(1)} %get-tuple-element.40), channel_id=1, source_target_pairs={{0,2},{1,3},{2,0},{3,1},{4,6},{5,7},{6,4},{7,5},{8,10},{9,11},{10,... | collective-permute-start | bytes 786440 | tf_op jit(solution)/shard_map/ppermute | solution.py:14
  7.6 19.7 %copy-start.20 = (pred[256,256]{0,1:T(8,128)(4,1)}, pred[256,256]{0,1:T(8,128)(4,1)S(1)}, u32[]{:S(2)}) copy-start(pred[256,256]{0,1:T(8,128)(4,1)S(1)} %fusion.28) | copy-start | bytes 196612
  7.7 19.7 %copy-start.33 = (f32[4,256]{1,0:T(4,128)}, f32[4,256]{1,0:T(4,128)S(1)}, u32[]{:S(2)}) copy-start(f32[4,256]{1,0:T(4,128)S(1)} %get-tuple-element.45) | copy-start | bytes 12292
  7.7 19.6 %copy-start.34 = (f32[4,256]{1,0:T(4,128)}, f32[4,256]{1,0:T(4,128)S(1)}, u32[]{:S(2)}) copy-start(f32[4,256]{1,0:T(4,128)S(1)} %get-tuple-element.48) | copy-start | bytes 12292
  7.7 19.6 %copy-start.35 = (f32[4,256]{1,0:T(4,128)}, f32[4,256]{1,0:T(4,128)S(1)}, u32[]{:S(2)}) copy-start(f32[4,256]{1,0:T(4,128)S(1)} %get-tuple-element.49) | copy-start | bytes 12292
  7.7 19.6 %copy-start.36 = (f32[4,256]{1,0:T(4,128)}, f32[4,256]{1,0:T(4,128)S(1)}, u32[]{:S(2)}) copy-start(f32[4,256]{1,0:T(4,128)S(1)} %get-tuple-element.50) | copy-start | bytes 12292
  7.7 19.6 %copy-start.37 = (f32[4,256]{1,0:T(4,128)}, f32[4,256]{1,0:T(4,128)S(1)}, u32[]{:S(2)}) copy-start(f32[4,256]{1,0:T(4,128)S(1)} %get-tuple-element.51) | copy-start | bytes 12292
  7.7 19.6 %copy-start.38 = (f32[4,256]{1,0:T(4,128)}, f32[4,256]{1,0:T(4,128)S(1)}, u32[]{:S(2)}) copy-start(f32[4,256]{1,0:T(4,128)S(1)} %get-tuple-element.52) | copy-start | bytes 12292
  7.8 19.6 %copy-start.39 = (f32[4,256]{1,0:T(4,128)}, f32[4,256]{1,0:T(4,128)S(1)}, u32[]{:S(2)}) copy-start(f32[4,256]{1,0:T(4,128)S(1)} %get-tuple-element.53) | copy-start | bytes 12292
  7.8 19.6 %copy-start.40 = (f32[4,256]{1,0:T(4,128)}, f32[4,256]{1,0:T(4,128)S(1)}, u32[]{:S(2)}) copy-start(f32[4,256]{1,0:T(4,128)S(1)} %get-tuple-element.54) | copy-start | bytes 12292
  7.8 19.6 %copy-start.41 = (f32[4,256]{1,0:T(4,128)}, f32[4,256]{1,0:T(4,128)S(1)}, u32[]{:S(2)}) copy-start(f32[4,256]{1,0:T(4,128)S(1)} %get-tuple-element.55) | copy-start | bytes 12292
  14.9 7.8 %collective-permute-start.2 = (f32[4,128,128]{2,1,0:T(8,128)S(1)}, f32[4,128,128]{2,1,0:T(8,128)S(1)}, u32[]{:S(2)}, u32[]{:S(2)}) collective-permute-start(f32[4,128,128]{2,1,0:T(8,128)S(1)} %get-tuple-element.42), channel_id=1, source_target_pairs={{0,4},{1,5},{2,6},{3,7},{4,0},{5,1},{6,2},{7,3},{8,12},{9,13},{10,... | collective-permute-start | bytes 786440 | tf_op jit(solution)/shard_map/ppermute | solution.py:14
  18.0 9.4 %copy-start.22 = (pred[256,256]{0,1:T(8,128)(4,1)}, pred[256,256]{0,1:T(8,128)(4,1)S(1)}, u32[]{:S(2)}) copy-start(pred[256,256]{0,1:T(8,128)(4,1)S(1)} %get-tuple-element.71) | copy-start | bytes 196612
  18.0 9.4 %copy-start.24 = (pred[256,256]{0,1:T(8,128)(4,1)}, pred[256,256]{0,1:T(8,128)(4,1)S(1)}, u32[]{:S(2)}) copy-start(pred[256,256]{0,1:T(8,128)(4,1)S(1)} %get-tuple-element.72) | copy-start | bytes 196612
  18.2 9.3 %copy-start.26 = (pred[256,256]{0,1:T(8,128)(4,1)}, pred[256,256]{0,1:T(8,128)(4,1)S(1)}, u32[]{:S(2)}) copy-start(pred[256,256]{0,1:T(8,128)(4,1)S(1)} %get-tuple-element.73) | copy-start | bytes 196612
  18.2 9.3 %copy-start.28 = (pred[256,256]{0,1:T(8,128)(4,1)}, pred[256,256]{0,1:T(8,128)(4,1)S(1)}, u32[]{:S(2)}) copy-start(pred[256,256]{0,1:T(8,128)(4,1)S(1)} %get-tuple-element.74) | copy-start | bytes 196612
  22.7 13.6 %copy-start.13 = (f32[1,4,128,128]{3,2,1,0:T(8,128)}, f32[1,4,128,128]{3,2,1,0:T(8,128)S(1)}, u32[]{:S(2)}) copy-start(f32[1,4,128,128]{3,2,1,0:T(8,128)S(1)} %get-tuple-element.43) | copy-start | bytes 786436
  22.7 13.5 %collective-permute-start.3 = (f32[4,128,128]{2,1,0:T(8,128)S(1)}, f32[4,128,128]{2,1,0:T(8,128)S(1)}, u32[]{:S(2)}, u32[]{:S(2)}) collective-permute-start(f32[4,128,128]{2,1,0:T(8,128)S(1)} %get-tuple-element.44), channel_id=1, source_target_pairs={{0,8},{1,9},{2,10},{3,11},{4,12},{5,13},{6,14},{7,15},{8,0},{9,1},... | collective-permute-start | bytes 786440 | tf_op jit(solution)/shard_map/ppermute | solution.py:14
  25.3 10.9 %copy-start.11 = (f32[1,4,128,128]{3,2,1,0:T(8,128)S(1)}, f32[1,4,128,128]{3,2,1,0:T(8,128)}, u32[]{:S(2)}) copy-start(f32[1,4,128,128]{3,2,1,0:T(8,128)} %get-tuple-element.41) | copy-start | bytes 786436
  27.5 9.9 %copy-start.4 = (bf16[4,256,256]{1,2,0:T(8,128)(2,1)}, bf16[4,256,256]{1,2,0:T(8,128)(2,1)S(1)}, u32[]{:S(2)}) copy-start(bf16[4,256,256]{1,2,0:T(8,128)(2,1)S(1)} %get-tuple-element.62) | copy-start | bytes 1572868
  36.2 2.4 %copy-start.7 = (f32[1,4,128,128]{3,2,1,0:T(8,128)}, f32[1,4,128,128]{3,2,1,0:T(8,128)S(1)}, u32[]{:S(2)}) copy-start(f32[1,4,128,128]{3,2,1,0:T(8,128)S(1)} %select_bitcast_fusion) | copy-start | bytes 786436
  36.2 1.2 %copy-start.32 = (f32[4,128]{1,0:T(4,128)S(1)}, f32[4,128]{1,0:T(4,128)}, u32[]{:S(2)}) copy-start(f32[4,128]{1,0:T(4,128)} %param.10) | copy-start | bytes 6148
  49.2 2.4 %copy-start.6 = (f32[4,256,256]{1,2,0:T(8,128)S(1)}, f32[4,256,256]{1,2,0:T(8,128)}, u32[]{:S(2)}) copy-start(f32[4,256,256]{1,2,0:T(8,128)} %get-tuple-element.63) | copy-start | bytes 3145732
  49.2 2.4 %copy-start.17 = (pred[256,256]{0,1:T(8,128)(4,1)S(1)}, pred[256,256]{0,1:T(8,128)(4,1)}, u32[]{:S(2)}) copy-start(pred[256,256]{0,1:T(8,128)(4,1)} %copy-done.16) | copy-start | bytes 196612
  49.2 2.4 %copy-start.19 = (pred[256,256]{0,1:T(8,128)(4,1)S(1)}, pred[256,256]{0,1:T(8,128)(4,1)}, u32[]{:S(2)}) copy-start(pred[256,256]{0,1:T(8,128)(4,1)} %copy-done.18) | copy-start | bytes 196612
  49.2 2.4 %copy-start.21 = (pred[256,256]{0,1:T(8,128)(4,1)S(1)}, pred[256,256]{0,1:T(8,128)(4,1)}, u32[]{:S(2)}) copy-start(pred[256,256]{0,1:T(8,128)(4,1)} %copy-done.20) | copy-start | bytes 196612
  49.2 2.4 %copy-start.23 = (pred[256,256]{0,1:T(8,128)(4,1)S(1)}, pred[256,256]{0,1:T(8,128)(4,1)}, u32[]{:S(2)}) copy-start(pred[256,256]{0,1:T(8,128)(4,1)} %copy-done.22) | copy-start | bytes 196612
  49.2 2.4 %copy-start.25 = (pred[256,256]{0,1:T(8,128)(4,1)S(1)}, pred[256,256]{0,1:T(8,128)(4,1)}, u32[]{:S(2)}) copy-start(pred[256,256]{0,1:T(8,128)(4,1)} %copy-done.24) | copy-start | bytes 196612
  49.2 2.4 %copy-start.27 = (pred[256,256]{0,1:T(8,128)(4,1)S(1)}, pred[256,256]{0,1:T(8,128)(4,1)}, u32[]{:S(2)}) copy-start(pred[256,256]{0,1:T(8,128)(4,1)} %copy-done.26) | copy-start | bytes 196612
  49.3 2.4 %copy-start.29 = (pred[256,256]{0,1:T(8,128)(4,1)S(1)}, pred[256,256]{0,1:T(8,128)(4,1)}, u32[]{:S(2)}) copy-start(pred[256,256]{0,1:T(8,128)(4,1)} %copy-done.28) | copy-start | bytes 196612
  51.6 1.0 %copy-start.3 = (f32[4,256,128]{1,2,0:T(8,128)S(1)}, f32[4,256,128]{1,2,0:T(8,128)}, u32[]{:S(2)}) copy-start(f32[4,256,128]{1,2,0:T(8,128)} %copy.42) | copy-start | bytes 1572868
  53.0 5.1 %copy-start.5 = (bf16[4,256,256]{1,2,0:T(8,128)(2,1)S(1)}, bf16[4,256,256]{1,2,0:T(8,128)(2,1)}, u32[]{:S(2)}) copy-start(bf16[4,256,256]{1,2,0:T(8,128)(2,1)} %copy-done.4) | copy-start | bytes 1572868
  53.8 1.5 %collective-permute-start.10 = (f32[4,128,128]{2,1,0:T(8,128)S(1)}, f32[4,128,128]{2,1,0:T(8,128)S(1)}, u32[]{:S(2)}, u32[]{:S(2)}) collective-permute-start(f32[4,128,128]{2,1,0:T(8,128)S(1)} %get-tuple-element.32), channel_id=1, source_target_pairs={{0,1},{1,0},{2,3},{3,2},{4,5},{5,4},{6,7},{7,6},{8,9},{9,8},{10,11... | collective-permute-start | bytes 786440 | tf_op jit(solution)/shard_map/ppermute | solution.py:14
  53.8 1.9 %collective-permute-start.5 = (f32[4,128,128]{2,1,0:T(8,128)S(1)}, f32[4,128,128]{2,1,0:T(8,128)S(1)}, u32[]{:S(2)}, u32[]{:S(2)}) collective-permute-start(f32[4,128,128]{2,1,0:T(8,128)S(1)} %get-tuple-element.34), channel_id=1, source_target_pairs={{0,1},{1,0},{2,3},{3,2},{4,5},{5,4},{6,7},{7,6},{8,9},{9,8},{10,11... | collective-permute-start | bytes 786440 | tf_op jit(solution)/shard_map/ppermute | solution.py:14
  54.3 1.8 %collective-permute-start.7 = (f32[4,128,128]{2,1,0:T(8,128)S(1)}, f32[4,128,128]{2,1,0:T(8,128)S(1)}, u32[]{:S(2)}, u32[]{:S(2)}) collective-permute-start(f32[4,128,128]{2,1,0:T(8,128)S(1)} %get-tuple-element.33), channel_id=1, source_target_pairs={{0,1},{1,0},{2,3},{3,2},{4,5},{5,4},{6,7},{7,6},{8,9},{9,8},{10,11... | collective-permute-start | bytes 786440 | tf_op jit(solution)/shard_map/ppermute | solution.py:14
  54.3 24.6 %collective-permute-start.4 = (f32[4,128,128]{2,1,0:T(8,128)}, f32[4,128,128]{2,1,0:T(8,128)}, u32[]{:S(2)}, u32[]{:S(2)}) collective-permute-start(f32[4,128,128]{2,1,0:T(8,128)} %get-tuple-element.31), channel_id=1, source_target_pairs={{0,1},{1,0},{2,3},{3,2},{4,5},{5,4},{6,7},{7,6},{8,9},{9,8},{10,11... | collective-permute-start | bytes 786440 | tf_op jit(solution)/shard_map/ppermute | solution.py:14
  55.0 11.6 %copy-start.8 = (f32[1,4,128,128]{3,2,1,0:T(8,128)S(1)}, f32[1,4,128,128]{3,2,1,0:T(8,128)}, u32[]{:S(2)}) copy-start(f32[1,4,128,128]{3,2,1,0:T(8,128)} %copy-done.7) | copy-start | bytes 786436
  55.0 11.6 %copy-start.10 = (f32[1,4,128,128]{3,2,1,0:T(8,128)S(1)}, f32[1,4,128,128]{3,2,1,0:T(8,128)}, u32[]{:S(2)}) copy-start(f32[1,4,128,128]{3,2,1,0:T(8,128)} %copy-done.9) | copy-start | bytes 786436
  55.0 11.6 %copy-start.12 = (f32[1,4,128,128]{3,2,1,0:T(8,128)S(1)}, f32[1,4,128,128]{3,2,1,0:T(8,128)}, u32[]{:S(2)}) copy-start(f32[1,4,128,128]{3,2,1,0:T(8,128)} %get-tuple-element.41) | copy-start | bytes 786436
  55.0 11.6 %copy-start.14 = (f32[1,4,128,128]{3,2,1,0:T(8,128)S(1)}, f32[1,4,128,128]{3,2,1,0:T(8,128)}, u32[]{:S(2)}) copy-start(f32[1,4,128,128]{3,2,1,0:T(8,128)} %copy-done.13) | copy-start | bytes 786436
  56.9 9.2 %collective-permute-start.11 = (f32[4,128,128]{2,1,0:T(8,128)S(1)}, f32[4,128,128]{2,1,0:T(8,128)S(1)}, u32[]{:S(2)}, u32[]{:S(2)}) collective-permute-start(f32[4,128,128]{2,1,0:T(8,128)S(1)} %get-tuple-element.36), channel_id=1, source_target_pairs={{0,2},{1,3},{2,0},{3,1},{4,6},{5,7},{6,4},{7,5},{8,10},{9,11},{10,... | collective-permute-start | bytes 786440 | tf_op jit(solution)/shard_map/ppermute | solution.py:14
  58.1 10.3 %copy-start.42 = (f32[4,13,256]{2,0,1:T(4,128)}, f32[4,13,256]{2,0,1:T(4,128)S(1)}, u32[]{:S(2)}) copy-start(f32[4,13,256]{2,0,1:T(4,128)S(1)} %constant_dynamic-update-slice_fusion) | copy-start | bytes 159748
  58.4 14.0 %collective-permute-start.8 = (f32[4,128,128]{2,1,0:T(8,128)S(1)}, f32[4,128,128]{2,1,0:T(8,128)}, u32[]{:S(2)}, u32[]{:S(2)}) collective-permute-start(f32[4,128,128]{2,1,0:T(8,128)S(1)} %get-tuple-element.37), channel_id=1, source_target_pairs={{0,2},{1,3},{2,0},{3,1},{4,6},{5,7},{6,4},{7,5},{8,10},{9,11},{10,... | collective-permute-start | bytes 786440 | tf_op jit(solution)/shard_map/ppermute | solution.py:14
  66.1 8.6 %collective-permute-start.12 = (f32[4,128,128]{2,1,0:T(8,128)S(1)}, f32[4,128,128]{2,1,0:T(8,128)}, u32[]{:S(2)}, u32[]{:S(2)}) collective-permute-start(f32[4,128,128]{2,1,0:T(8,128)S(1)} %add.371), channel_id=1, source_target_pairs={{0,4},{1,5},{2,6},{3,7},{4,0},{5,1},{6,2},{7,3},{8,12},{9,13},{10,... | collective-permute-start | bytes 786440 | tf_op jit(solution)/shard_map/ppermute | solution.py:14
  68.4 2.4 %copy-start.15 = (f32[4,128,128]{2,1,0:T(8,128)S(1)}, f32[4,128,128]{2,1,0:T(8,128)}, u32[]{:S(2)}) copy-start(f32[4,128,128]{2,1,0:T(8,128)} %get-tuple-element.35) | copy-start | bytes 786436
  70.8 8.1 %collective-permute-start.6 = (f32[4,128,128]{2,1,0:T(8,128)S(1)}, f32[4,128,128]{2,1,0:T(8,128)S(1)}, u32[]{:S(2)}, u32[]{:S(2)}) collective-permute-start(f32[4,128,128]{2,1,0:T(8,128)S(1)} %copy-done.15), channel_id=1, source_target_pairs={{0,2},{1,3},{2,0},{3,1},{4,6},{5,7},{6,4},{7,5},{8,10},{9,11},{10,... | collective-permute-start | bytes 786440 | tf_op jit(solution)/shard_map/ppermute | solution.py:14
  73.4 11.4 %collective-permute-start.9 = (f32[4,128,128]{2,1,0:T(8,128)S(1)}, f32[4,128,128]{2,1,0:T(8,128)S(1)}, u32[]{:S(2)}, u32[]{:S(2)}) collective-permute-start(f32[4,128,128]{2,1,0:T(8,128)S(1)} %add.368), channel_id=1, source_target_pairs={{0,4},{1,5},{2,6},{3,7},{4,0},{5,1},{6,2},{7,3},{8,12},{9,13},{10,... | collective-permute-start | bytes 786440 | tf_op jit(solution)/shard_map/ppermute | solution.py:14
  75.8 12.4 %collective-permute-start.13 = (f32[4,128,128]{2,1,0:T(8,128)S(1)}, f32[4,128,128]{2,1,0:T(8,128)S(1)}, u32[]{:S(2)}, u32[]{:S(2)}) collective-permute-start(f32[4,128,128]{2,1,0:T(8,128)S(1)} %add.372), channel_id=1, source_target_pairs={{0,8},{1,9},{2,10},{3,11},{4,12},{5,13},{6,14},{7,15},{8,0},{9,1},... | collective-permute-start | bytes 786440 | tf_op jit(solution)/shard_map/ppermute | solution.py:14
